TPU v7x, 32 devices: a whole 2x2x4 slice. The times are simulated.
32 devices in a mesh: tm: 8 (over z, core), space: 4 (over y, x).
Axes of the slice: x: 2, y: 2, z: 4, core: 2. Of those that a mesh axis runs over, the one named last changes fastest.
Arguments:
- snapshots: bfloat16 [4096, 12288], P('tm', 'space')
- freq_ids: int32 [64], replicated, may hold values from 0 to 127
Outputs:
- gram: float32 [64, 2, 15, 15], P('tm')
All inputs are finite; a program needn't handle non-finite values.
Results may differ from a plain program's by a relative error of at most 0.00039.
Values may be sent and summed in bfloat16 or wider, within the bound.
No kernel may reach another device: no remote copies, remote signals or barrier semaphores. Data moves between devices by JAX's collectives and lax.ppermute only.
A program may use at most 64 MiB of HBM per device.

v0:
```python
import math
import jax
import jax.numpy as jnp
from jax import lax
from jax.sharding import PartitionSpec as P

NFFT = 512
F = 64


def shifted(block, axis, distance):
    devices = range(lax.axis_size(axis))
    route = [(i - distance, i) for i in devices if i - distance in devices]
    return lax.ppermute(block, axis, route)


def kernel_values(freqs, shifts, window_length):
    phase = freqs * shifts % window_length
    angle = 2.0 * math.pi / window_length * phase.astype(jnp.float32)
    window = 0.5 - 0.5 * jnp.cos(2.0 * math.pi / window_length * shifts.astype(jnp.float32))
    return (window * jnp.cos(angle), -window * jnp.sin(angle))


def local(snapshots, freq_ids):
    hop_len = NFFT // 2
    count_tm = lax.axis_size("tm")
    blocks = 2 * count_tm - 1
    device = lax.axis_index("tm")
    points = snapshots.shape[1]
    shifts = jnp.arange(NFFT, dtype=jnp.int32)
    real_part, imag_part = kernel_values(freq_ids[:, None], shifts[None, :], NFFT)
    table = jnp.stack([real_part, imag_part], axis=1).reshape(2 * F, NFFT).astype(jnp.bfloat16)
    leading = shifted(snapshots[:hop_len], "tm", -1)
    extended = jnp.concatenate([snapshots, leading], axis=0)
    pieces = []
    for slot in range(2):
        block = device * 2 + slot
        segment = extended[hop_len * slot : hop_len * slot + NFFT]
        result = jnp.dot(table, segment, preferred_element_type=jnp.float32)
        pieces.append(jnp.where(block < blocks, result, 0.0))
    owned = jnp.stack(pieces, axis=0).astype(jnp.bfloat16)
    owned = owned.reshape(2, F, 2, points)
    by_freq = lax.all_to_all(owned, "tm", split_axis=1, concat_axis=0, tiled=True)
    slots_all = by_freq.shape[0]
    resident_frequencies = by_freq.shape[1]
    stacked_snapshot_rows = jnp.transpose(by_freq, (1, 2, 0, 3)).reshape(
        resident_frequencies, 2 * slots_all, points
    )
    cross_product_terms = jnp.einsum(
        "tnf,tof->tno",
        stacked_snapshot_rows,
        stacked_snapshot_rows,
        preferred_element_type=jnp.float32,
    )
    gram_real_matrix = (
        cross_product_terms[:, :slots_all, :slots_all]
        + cross_product_terms[:, slots_all:, slots_all:]
    )
    imag_gram = (
        cross_product_terms[:, slots_all:, :slots_all]
        - cross_product_terms[:, :slots_all, slots_all:]
    )
    scale = 1.0 / (NFFT * points * lax.axis_size("space"))
    resident_gram_matrix = (
        jnp.stack([gram_real_matrix, imag_gram], axis=1)[:, :, :blocks, :blocks] * scale
    )
    return lax.psum(resident_gram_matrix, "space")


def solution(mesh):
    return jax.shard_map(
        local,
        mesh=mesh,
        in_specs=(P("tm", "space"), P()),
        out_specs=P("tm", None, None, None),
        check_vma=False,
    )
```

profile of v0, /device:TPU:0, one launch (start us, length us, event | category | flops | bytes accessed | tf_op | source)
XLA Modules:
  0.0 96.8 jit_solution(8468911311742353693)
XLA Ops:
  0.0 0.0 copy-start
  0.0 0.0 copy-start.2
  0.0 2.8 %slice.21 = bf16[256,3072]{1,0:T(8,128)(2,1)} slice(bf16[512,3072]{1,0:T(8,128)(2,1)} %param.2), slice={[0:256], [0:3072]} | slice | bytes 3145728 | tf_op jit(solution)/shard_map/slice | solution.py:33
  2.8 1.3 %collective-permute-start = (bf16[256,3072]{1,0:T(8,128)(2,1)}, bf16[256,3072]{1,0:T(8,128)(2,1)}, u32[]{:S(2)}, u32[]{:S(2)}) collective-permute-start(bf16[256,3072]{1,0:T(8,128)(2,1)} %slice.21), channel_id=1, source_target_pairs={{4,0},{8,4},{12,8},{16,12},{20,16},{24,20},{28,24},{5,1},{9,5},{13... | collective-permute-start | bytes 4718600 | tf_op jit(solution)/shard_map/ppermute | solution.py:14
  4.2 0.0 copy-done.2
  4.2 0.6 multiply_convert_fusion.1
  4.8 0.1 copy.13
  5.0 0.1 convert_element_type.35
  5.0 0.0 copy-done
  5.0 1.5 %fusion = bf16[128,3072]{1,0:T(8,128)(2,1)} fusion(bf16[128,512]{1,0:T(8,128)(2,1)S(1)} %convert_element_type.35, bf16[512,3072]{1,0:T(8,128)(2,1)S(1)} %copy-done, pred[]{:T(512)S(6)} %lt.12), kind=kOutput, calls=%fused_computation.2 | convolution fusion | flops 403439616 | bytes 4063233 | tf_op jit(solution)/shard_map/dot_general | solution.py:39
  6.5 2.8 %stack.25 = bf16[1,64,2,3072]{3,2,1,0:T(2,128)(2,1)} reshape(bf16[128,3072]{1,0:T(8,128)(2,1)} %fusion) | data formatting | bytes 1572864 | tf_op jit(solution)/shard_map/stack | solution.py:41
  9.4 0.0 collective-permute-done
  9.4 2.9 %fusion.1 = bf16[128,3072]{1,0:T(8,128)(2,1)} fusion(bf16[128,512]{1,0:T(8,128)(2,1)S(1)} %convert_element_type.35, bf16[256,3072]{1,0:T(8,128)(2,1)} %collective-permute-done, bf16[512,3072]{1,0:T(8,128)(2,1)S(1)} %copy-done, pred[]{:T(512)S(6)} %lt.14), kind=kOutput, calls=%fused_computation.3 | convolution fusion | flops 409731072 | bytes 5636097 | tf_op jit(solution)/shard_map/dot_general | solution.py:39
  12.3 0.0 copy-start.1
  12.3 2.2 %stack.26 = bf16[1,64,2,3072]{3,2,1,0:T(2,128)(2,1)S(1)} reshape(bf16[128,3072]{1,0:T(8,128)(2,1)} %fusion.1) | data formatting | bytes 1572864 | tf_op jit(solution)/shard_map/stack | solution.py:41
  14.5 0.0 copy-done.1
  14.5 2.1 %pad_maximum_fusion.2 = bf16[2,64,2,3072]{3,2,0,1:T(2,128)(2,1)S(1)} fusion(bf16[1,64,2,3072]{3,2,0,1:T(2,128)(2,1)S(1)} %bitcast.22, bf16[1,64,2,3072]{3,2,0,1:T(2,128)(2,1)S(1)} %bitcast.21), kind=kLoop, calls=%fused_computation.6 | loop fusion | flops 786432 | bytes 3145728 | tf_op jit(solution)/shard_map/stack | solution.py:41
  16.6 58.0 %all_to_all.18 = bf16[2,64,2,3072]{3,2,0,1:T(2,128)(2,1)S(1)} all-to-all(bf16[2,64,2,3072]{3,2,0,1:T(2,128)(2,1)S(1)} %pad_maximum_fusion.2), channel_id=1, replica_groups=mesh['tm'=8,'space'=4] {'tm'}, dimensions={1} | all-to-all | bytes 3145728 | tf_op jit(solution)/shard_map/all_to_all | solution.py:43
  74.6 1.7 %copy.16 = bf16[8,2,8,2,3072]{4,1,0,3,2:T(2,128)(2,1)S(1)} copy(bf16[8,2,8,2,3072]{4,3,1,2,0:T(2,128)(2,1)S(1)} %bitcast.20) | data formatting | bytes 3145728 | tf_op jit(solution)/shard_map/all_to_all | solution.py:43
  76.3 0.6 all_to_all.16
  76.9 0.5 fusion.14
  77.5 0.1 fusion.11
  77.6 18.4 %psum.7 = f32[8,2,15,15]{3,2,0,1:T(8,128)S(1)} all-reduce(f32[8,2,15,15]{3,2,0,1:T(8,128)S(1)} %fusion.6), channel_id=1, replica_groups=mesh['tm'=8,'space'=4] {'space'}, use_global_device_ids=true, to_apply=%region_0.1 | all-reduce | flops 3600 | bytes 28800 | tf_op jit(solution)/shard_map/psum | solution.py:67
  96.0 0.7 copy.17
  (3 shorter events, 0.1 us)
Async XLA Ops:
  0.0 5.0 %copy-start = (bf16[512,3072]{1,0:T(8,128)(2,1)S(1)}, bf16[512,3072]{1,0:T(8,128)(2,1)}, u32[]{:S(2)}) copy-start(bf16[512,3072]{1,0:T(8,128)(2,1)} %param.2) | copy-start | bytes 9437188
  0.0 4.2 %copy-start.2 = (s32[64]{0:T(128)S(1)}, s32[64]{0:T(128)}, u32[]{:S(2)}) copy-start(s32[64]{0:T(128)} %param.3) | copy-start | bytes 772
  2.8 6.5 %collective-permute-start = (bf16[256,3072]{1,0:T(8,128)(2,1)}, bf16[256,3072]{1,0:T(8,128)(2,1)}, u32[]{:S(2)}, u32[]{:S(2)}) collective-permute-start(bf16[256,3072]{1,0:T(8,128)(2,1)} %slice.21), channel_id=1, source_target_pairs={{4,0},{8,4},{12,8},{16,12},{20,16},{24,20},{28,24},{5,1},{9,5},{13... | collective-permute-start | bytes 4718600 | tf_op jit(solution)/shard_map/ppermute | solution.py:14
  12.3 2.2 %copy-start.1 = (bf16[1,64,2,3072]{3,2,1,0:T(2,128)(2,1)S(1)}, bf16[1,64,2,3072]{3,2,1,0:T(2,128)(2,1)}, u32[]{:S(2)}) copy-start(bf16[1,64,2,3072]{3,2,1,0:T(2,128)(2,1)} %stack.25) | copy-start | bytes 2359300
where the time goes:
time: 97 us; the launch traced here: 96.8 us
  blocking collectives  76.4 us (79%)
  local copies, waits for them, and re-layouts  11.2 us (12%)
  matrix products  4.92 us (5%)
  other arithmetic  2.86 us (3%)
  starting transfers between devices  1.28 us (1%)
    all_to_all x1, blocking collectives, local(): lax.all_to_all(owned, 'tm', split_axis=1, concat_axis=0, tiled=True)  58 us
    psum x1, blocking collectives, local(): return lax.psum(resident_gram_matrix, 'space')  18.4 us
    another operation x2, local copies, waits for them, and re-layouts, local(): owned = jnp.stack(pieces, axis=0).astype(jnp.bfloat16)  5.07 us
    dot_general x2, matrix products, local(): result = jnp.dot(table, segment, preferred_element_type=jnp.float32)  4.38 us
    slice x1, local copies, waits for them, and re-layouts, local(): leading = shifted(snapshots[:hop_len], 'tm', -1)  2.83 us
    all_to_all x2, local copies, waits for them, and re-layouts, local(): lax.all_to_all(owned, 'tm', split_axis=1, concat_axis=0, tiled=True)  2.33 us
    another operation x1, other arithmetic, local(): owned = jnp.stack(pieces, axis=0).astype(jnp.bfloat16)  2.07 us
  transfers between devices with their start and end apart: 1, of which 0 were waited for; matrix products, arithmetic and copies ran while one was open for 5% of the time, Pallas kernels for 0%

commit v1 on v0

--- a/solution.py
+++ b/solution.py
@@ -64,7 +64,7 @@
     resident_gram_matrix = (
         jnp.stack([gram_real_matrix, imag_gram], axis=1)[:, :, :blocks, :blocks] * scale
     )
-    return lax.psum(resident_gram_matrix, "space")
+    return jnp.sum(lax.all_gather(resident_gram_matrix, "space"), axis=0)
 
 
 def solution(mesh):

time: 97 us -> 88.7 us (0.914)
  blocking collectives: 76.4 us -> 68.1 us
    psum x1 -> x0, blocking collectives: 18.4 us -> none  [local(): return lax.psum(resident_gram_matrix, 'space')]
    all_gather x0 -> x1, blocking collectives: none -> 10 us  [local(): return jnp.sum(lax.all_gather(resident_gram_matrix, 'space'), axis=0)]
  transfers between devices with their start and end apart: 1 -> 1, of which waited for: 0 -> 0; matrix products, arithmetic and copies ran while one was open for 5% -> 6% of each run, Pallas kernels for 0% -> 0%
where the time goes in v1:
time: 88.7 us; the launch traced here: 88.5 us
  blocking collectives  68.1 us (77%)
  local copies, waits for them, and re-layouts  11.2 us (13%)
  matrix products  4.92 us (6%)
  other arithmetic  2.91 us (3%)
  starting transfers between devices  1.28 us (1%)
    all_to_all x1, blocking collectives, local(): lax.all_to_all(owned, 'tm', split_axis=1, concat_axis=0, tiled=True)  58 us
    all_gather x1, blocking collectives, local(): return jnp.sum(lax.all_gather(resident_gram_matrix, 'space'), axis=0)  10 us
    another operation x2, local copies, waits for them, and re-layouts, local(): owned = jnp.stack(pieces, axis=0).astype(jnp.bfloat16)  5.07 us
    dot_general x2, matrix products, local(): result = jnp.dot(table, segment, preferred_element_type=jnp.float32)  4.38 us
    slice x1, local copies, waits for them, and re-layouts, local(): leading = shifted(snapshots[:hop_len], 'tm', -1)  2.83 us
    all_to_all x2, local copies, waits for them, and re-layouts, local(): lax.all_to_all(owned, 'tm', split_axis=1, concat_axis=0, tiled=True)  2.33 us
    another operation x1, other arithmetic, local(): owned = jnp.stack(pieces, axis=0).astype(jnp.bfloat16)  2.07 us
  transfers between devices with their start and end apart: 1, of which 0 were waited for; matrix products, arithmetic and copies ran while one was open for 6% of the time, Pallas kernels for 0%

profile of v1, /device:TPU:0, one launch (start us, length us, event | category | flops | bytes accessed | tf_op | source)
XLA Modules:
  0.0 88.5 jit_solution(4166234434622462124)
XLA Ops:
  0.0 0.0 copy-start
  0.0 0.0 copy-start.2
  0.0 2.8 %slice.21 = bf16[256,3072]{1,0:T(8,128)(2,1)} slice(bf16[512,3072]{1,0:T(8,128)(2,1)} %param.2), slice={[0:256], [0:3072]} | slice | bytes 3145728 | tf_op jit(solution)/shard_map/slice | solution.py:33
  2.8 1.3 %collective-permute-start = (bf16[256,3072]{1,0:T(8,128)(2,1)}, bf16[256,3072]{1,0:T(8,128)(2,1)}, u32[]{:S(2)}, u32[]{:S(2)}) collective-permute-start(bf16[256,3072]{1,0:T(8,128)(2,1)} %slice.21), channel_id=1, source_target_pairs={{4,0},{8,4},{12,8},{16,12},{20,16},{24,20},{28,24},{5,1},{9,5},{13... | collective-permute-start | bytes 4718600 | tf_op jit(solution)/shard_map/ppermute | solution.py:14
  4.2 0.0 copy-done.2
  4.2 0.6 multiply_convert_fusion.1
  4.8 0.1 copy.12
  5.0 0.1 convert_element_type.35
  5.0 0.0 copy-done
  5.0 1.5 %fusion = bf16[128,3072]{1,0:T(8,128)(2,1)} fusion(bf16[128,512]{1,0:T(8,128)(2,1)S(1)} %convert_element_type.35, bf16[512,3072]{1,0:T(8,128)(2,1)S(1)} %copy-done, pred[]{:T(512)S(6)} %lt.12), kind=kOutput, calls=%fused_computation.2 | convolution fusion | flops 403439616 | bytes 4063233 | tf_op jit(solution)/shard_map/dot_general | solution.py:39
  6.5 2.8 %stack.25 = bf16[1,64,2,3072]{3,2,1,0:T(2,128)(2,1)} reshape(bf16[128,3072]{1,0:T(8,128)(2,1)} %fusion) | data formatting | bytes 1572864 | tf_op jit(solution)/shard_map/stack | solution.py:41
  9.4 0.0 collective-permute-done
  9.4 2.9 %fusion.1 = bf16[128,3072]{1,0:T(8,128)(2,1)} fusion(bf16[128,512]{1,0:T(8,128)(2,1)S(1)} %convert_element_type.35, bf16[256,3072]{1,0:T(8,128)(2,1)} %collective-permute-done, bf16[512,3072]{1,0:T(8,128)(2,1)S(1)} %copy-done, pred[]{:T(512)S(6)} %lt.14), kind=kOutput, calls=%fused_computation.3 | convolution fusion | flops 409731072 | bytes 5636097 | tf_op jit(solution)/shard_map/dot_general | solution.py:39
  12.3 0.0 copy-start.1
  12.3 2.2 %stack.26 = bf16[1,64,2,3072]{3,2,1,0:T(2,128)(2,1)S(1)} reshape(bf16[128,3072]{1,0:T(8,128)(2,1)} %fusion.1) | data formatting | bytes 1572864 | tf_op jit(solution)/shard_map/stack | solution.py:41
  14.5 0.0 copy-done.1
  14.5 2.1 %pad_maximum_fusion.2 = bf16[2,64,2,3072]{3,2,0,1:T(2,128)(2,1)S(1)} fusion(bf16[1,64,2,3072]{3,2,0,1:T(2,128)(2,1)S(1)} %bitcast.23, bf16[1,64,2,3072]{3,2,0,1:T(2,128)(2,1)S(1)} %bitcast.22), kind=kLoop, calls=%fused_computation.6 | loop fusion | flops 786432 | bytes 3145728 | tf_op jit(solution)/shard_map/stack | solution.py:41
  16.6 58.0 %all_to_all.18 = bf16[2,64,2,3072]{3,2,0,1:T(2,128)(2,1)S(1)} all-to-all(bf16[2,64,2,3072]{3,2,0,1:T(2,128)(2,1)S(1)} %pad_maximum_fusion.2), channel_id=1, replica_groups=mesh['tm'=8,'space'=4] {'tm'}, dimensions={1} | all-to-all | bytes 3145728 | tf_op jit(solution)/shard_map/all_to_all | solution.py:43
  74.6 1.7 %copy.15 = bf16[8,2,8,2,3072]{4,1,0,3,2:T(2,128)(2,1)S(1)} copy(bf16[8,2,8,2,3072]{4,3,1,2,0:T(2,128)(2,1)S(1)} %bitcast.21) | data formatting | bytes 3145728 | tf_op jit(solution)/shard_map/all_to_all | solution.py:43
  76.3 0.6 all_to_all.16
  76.9 0.5 fusion.14
  77.5 0.1 fusion.11
  77.6 10.0 %all-gather = f32[32,2,15,15]{3,2,0,1:T(8,128)S(1)} all-gather(f32[8,2,15,15]{3,2,0,1:T(8,128)S(1)} %fusion.6), channel_id=2, replica_groups=mesh['tm'=8,'space'=4] {'space'}, dimensions={0}, use_global_device_ids=true | all-gather | bytes 72000 | tf_op jit(solution)/shard_map/all_gather | solution.py:67
  87.7 0.1 reduce_sum.9
  87.7 0.7 copy.16
  (3 shorter events, 0.1 us)
Async XLA Ops:
  0.0 5.0 %copy-start = (bf16[512,3072]{1,0:T(8,128)(2,1)S(1)}, bf16[512,3072]{1,0:T(8,128)(2,1)}, u32[]{:S(2)}) copy-start(bf16[512,3072]{1,0:T(8,128)(2,1)} %param.2) | copy-start | bytes 9437188
  0.0 4.2 %copy-start.2 = (s32[64]{0:T(128)S(1)}, s32[64]{0:T(128)}, u32[]{:S(2)}) copy-start(s32[64]{0:T(128)} %param.3) | copy-start | bytes 772
  2.8 6.5 %collective-permute-start = (bf16[256,3072]{1,0:T(8,128)(2,1)}, bf16[256,3072]{1,0:T(8,128)(2,1)}, u32[]{:S(2)}, u32[]{:S(2)}) collective-permute-start(bf16[256,3072]{1,0:T(8,128)(2,1)} %slice.21), channel_id=1, source_target_pairs={{4,0},{8,4},{12,8},{16,12},{20,16},{24,20},{28,24},{5,1},{9,5},{13... | collective-permute-start | bytes 4718600 | tf_op jit(solution)/shard_map/ppermute | solution.py:14
  12.3 2.2 %copy-start.1 = (bf16[1,64,2,3072]{3,2,1,0:T(2,128)(2,1)S(1)}, bf16[1,64,2,3072]{3,2,1,0:T(2,128)(2,1)}, u32[]{:S(2)}) copy-start(bf16[1,64,2,3072]{3,2,1,0:T(2,128)(2,1)} %stack.25) | copy-start | bytes 2359300
